TPU v7x, 32 devices: a whole 2x2x4 slice. The times are simulated.
32 devices in a mesh: seq: 16 (over z, y, core), head: 2 (over x).
Axes of the slice: x: 2, y: 2, z: 4, core: 2. Of those that a mesh axis runs over, the one named last changes fastest.
Arguments:
- queries: bfloat16 [4, 64, 64, 128], P(None, None, 'head'), may hold values from -15 to 15
- new_keys: bfloat16 [4, 64, 8, 128], P(None, None, 'head'), may hold values from -16 to 16
- new_values: bfloat16 [4, 64, 8, 128], P(None, None, 'head'), may hold values from -6 to 6
- cache_keys: bfloat16 [4, 32768, 8, 128], P(None, 'seq', 'head'), may hold values from -6 to 6
- cache_values: bfloat16 [4, 32768, 8, 128], P(None, 'seq', 'head'), may hold values from -6 to 6
- parents: int32 [4, 64], replicated, may hold values from 0 to 63, as said below
- kv_lengths: int32 [4], replicated, may hold values from 1 to 32768
- out_weight: bfloat16 [8192, 8192], P('head', 'seq'), may hold values from -0.5 to 0.5
Outputs:
- mixed: bfloat16 [256, 8192], P('head', 'seq')
Inputs may be any that keep to these rules, and one draw needn't show every extreme that they name: parents[r, 0] = 0 for the root; for i >= 1, parents[r, i] < i.
All inputs are finite; a program needn't handle non-finite values.
Results may differ from a plain program's by a relative error of at most 0.0045.
Values may be sent and summed in bfloat16 or wider, within the bound.
A program may use at most 128 MiB of HBM per device.

v0:
```python
import math
import jax
import jax.numpy as jnp
from jax import lax
from jax.sharding import PartitionSpec as P

lowest = -1e30


def ancestors(parent_row):
    tree_size = parent_row.shape[0]
    indices = jnp.arange(tree_size, dtype=jnp.int32)
    parent_link = (parent_row[:, None] == indices[None, :]).astype(jnp.float32)
    itself = (indices[:, None] == indices[None, :]).astype(jnp.float32)
    reached = jnp.maximum(parent_link, itself)
    for repeat in range(max(1, (tree_size - 1).bit_length())):
        reached = jnp.minimum(jnp.dot(reached, reached, precision=lax.Precision.HIGHEST), 1.0)
    return reached


def partial_scores(query_rows, keys, values, allowed, score_scale):
    scores = (
        jnp.einsum("kqd,pkd->kqp", query_rows, keys, preferred_element_type=jnp.float32)
        * score_scale
    )
    scores = jnp.where(allowed, scores, lowest)
    maxima = jnp.max(scores, axis=-1)
    weights = jnp.where(allowed, jnp.exp(scores - maxima[..., None]), 0.0)
    totals = jnp.sum(weights, axis=-1)
    weighted = jnp.einsum(
        "kqp,pkd->kqd", weights.astype(jnp.bfloat16), values, preferred_element_type=jnp.float32
    )
    return (maxima, totals, weighted)


def body(queries, new_keys, new_values, cache_keys, cache_values, parents, kv_lengths, out_weight):
    requests, tree_size, heads, head_size = queries.shape
    kv_heads = new_keys.shape[2]
    group_size = heads // kv_heads
    block_size = cache_keys.shape[1]
    score_scale = 1.0 / math.sqrt(head_size)
    tokens = requests * tree_size
    positions = lax.axis_index("seq") * block_size + jnp.arange(block_size, dtype=jnp.int32)

    def token_order(maxima, totals, weighted):
        maxima = (
            maxima.reshape(kv_heads, tree_size, group_size)
            .transpose(1, 0, 2)
            .reshape(tree_size, heads)
        )
        totals = (
            totals.reshape(kv_heads, tree_size, group_size)
            .transpose(1, 0, 2)
            .reshape(tree_size, heads)
        )
        weighted = weighted.reshape(kv_heads, tree_size, group_size, head_size).transpose(
            1, 0, 2, 3
        )
        return (maxima, totals, weighted.reshape(tree_size, heads, head_size))

    def one_request(request_items):
        query, tree_keys, tree_values, past_keys, past_values, parent_row, length = request_items
        query_rows = query.reshape(tree_size, kv_heads, group_size, head_size).transpose(1, 0, 2, 3)
        query_rows = query_rows.reshape(kv_heads, tree_size * group_size, head_size)
        cache_max, cache_tot, cache_acc = partial_scores(
            query_rows, past_keys, past_values, positions < length, score_scale
        )
        tree_allowed = jnp.repeat(ancestors(parent_row), group_size, axis=0) > 0.5
        tree_max, tree_tot, tree_acc = partial_scores(
            query_rows, tree_keys, tree_values, tree_allowed, score_scale
        )
        return (
            token_order(cache_max, cache_tot, cache_acc),
            token_order(tree_max, tree_tot, tree_acc),
        )

    cache_part, tree_part = lax.map(
        one_request, (queries, new_keys, new_values, cache_keys, cache_values, parents, kv_lengths)
    )
    cache_max = cache_part[0].reshape(tokens, heads)
    cache_tot = cache_part[1].reshape(tokens, heads)
    cache_acc = cache_part[2].reshape(tokens, heads, head_size)
    tree_max = tree_part[0].reshape(tokens, heads)
    tree_tot = tree_part[1].reshape(tokens, heads)
    tree_acc = tree_part[2].reshape(tokens, heads, head_size)
    overall = lax.pmax(cache_max, "seq")
    overall = jnp.maximum(overall, tree_max)
    factor = jnp.exp(cache_max - overall)
    shared_acc, shared_tot = (
        lax.psum_scatter(cache_acc * factor[..., None], "seq", scatter_dimension=0, tiled=True),
        lax.psum_scatter(cache_tot * factor, "seq", scatter_dimension=0, tiled=True),
    )
    row_count = tokens // lax.axis_size("seq")
    first_row = lax.axis_index("seq") * row_count

    def take_rows(array):
        return lax.dynamic_slice_in_dim(array, first_row, row_count, 0)

    tree_factor = jnp.exp(take_rows(tree_max) - take_rows(overall))
    weighted = shared_acc + take_rows(tree_acc) * tree_factor[..., None]
    totals = shared_tot + take_rows(tree_tot) * tree_factor
    share = (
        (weighted / totals[..., None]).astype(jnp.bfloat16).reshape(row_count, heads * head_size)
    )
    attended = lax.all_gather(share, "seq", axis=0, tiled=True)
    mixed = lax.psum_scatter(
        jnp.dot(attended, out_weight, preferred_element_type=jnp.float32),
        "head",
        scatter_dimension=0,
        tiled=True,
    )
    return mixed.astype(jnp.bfloat16)


def solution(mesh):
    placed = (
        P(None, None, "head", None),
        P(None, None, "head", None),
        P(None, None, "head", None),
        P(None, "seq", "head", None),
        P(None, "seq", "head", None),
        P(),
        P(),
        P("head", "seq"),
    )
    return jax.shard_map(
        body, mesh=mesh, in_specs=placed, out_specs=P("head", "seq"), check_vma=False
    )
```

profile of v0, /device:TPU:0, one launch (start us, length us, event | category | flops | bytes accessed | tf_op | source)
XLA Modules:
  0.0 414.5 jit_solution(2779970047454667348)
XLA Ops:
  6.5 145.8 %while.21 = (s32[]{:T(128)}, f32[4,64,32]{1,0,2:T(4,128)S(1)}, f32[4,64,32]{1,0,2:T(4,128)S(1)}, f32[4,64,32,128]{3,2,1,0:T(8,128)}, f32[4,64,32]{1,0,2:T(4,128)...) while((s32[]{:T(128)}, f32[4,64,32]{1,0,2:T(4,128)S(1)}, ...), condition=%wide.region_5.6_spmd.clone, body=%wide.region_0.5_spmd.clone.sunk | while | flops 2289217536 | bytes 81249280 | solution.py:77
  6.6 1.5 dynamic_slice.82
  8.0 0.7 add_compare_fusion.2
  8.7 2.0 constant_dynamic-slice_fusion.9
  10.7 7.2 %fusion.81 = (f32[4,512]{1,0:T(4,128)S(1)}, f32[4,512,2048]{2,1,0:T(8,128)}) fusion(pred[2048]{0:T(1024)(128)(4,1)S(1)} %add_compare_fusion.2, bf16[1,2048,4,128]{3,2,1,0:T(4,128)(2,1)S(1)} %constant_dynamic-slice_fusion.9, bf16[4,64,32,128]{3,2,1,0:T(8,128)(2,1)S(1)} %copy-done, s32[]{:T(128)S(6)} %copy.150), kind=kOutput, calls=%fused_computation.3.clone.1 | convolution fusion | flops 1086322688 | bytes 19408900 | tf_op jit(solution)/shard_map/while/body/eval_jaxpr/kqd,pkd->kqp/dot_general | solution.py:23
  18.2 8.1 %fusion.82 = f32[4,512]{1,0:T(4,128)S(1)} fusion(f32[4,512,2048]{2,1,0:T(8,128)} %get-tuple-element.325, f32[4,512]{1,0:T(4,128)S(1)} %get-tuple-element.324, pred[2048]{0:T(1024)(128)(4,1)S(1)} %add_compare_fusion.2), kind=kLoop, calls=%fused_computation.5.clone.1 | loop fusion | flops 20969472 | bytes 16795648 | tf_op jit(solution)/shard_map/while/body/eval_jaxpr/reduce_sum | solution.py:29
  26.6 0.9 constant_dynamic-slice_fusion.10
  27.5 0.7 fusion.83
  29.4 0.3 fusion.85
  29.8 0.9 constant_dynamic-slice_fusion.11
  30.6 0.4 convolution_bitcast_fusion.2
  31.0 2.0 constant_dynamic-slice_fusion.12
  33.0 7.7 %fusion.86 = f32[64,4,8,128]{3,2,0,1:T(8,128)S(1)} fusion(bf16[1,2048,4,128]{3,2,1,0:T(4,128)(2,1)S(1)} %constant_dynamic-slice_fusion.12, f32[4,512,2048]{2,1,0:T(8,128)} %get-tuple-element.325, f32[4,512]{1,0:T(4,128)S(1)} %get-tuple-element.324, pred[2048]{0:T(1024)(128)(4,1)S(1)} %add_compare_fusion.2), kind=kOutput, calls=%fused_computation.11.clone.1 | convolution fusion | flops 1094713344 | bytes 19933184 | tf_op jit(solution)/shard_map/while/body/eval_jaxpr/kqp,pkd->kqd/dot_general | solution.py:30
  40.7 1.6 bitcast_dynamic-update-slice_fusion.3
  43.0 1.5 dynamic_slice.82
  44.5 0.7 add_compare_fusion.2
  45.2 2.0 constant_dynamic-slice_fusion.9
  47.2 7.2 %fusion.81 = (f32[4,512]{1,0:T(4,128)S(1)}, f32[4,512,2048]{2,1,0:T(8,128)}) fusion(pred[2048]{0:T(1024)(128)(4,1)S(1)} %add_compare_fusion.2, bf16[1,2048,4,128]{3,2,1,0:T(4,128)(2,1)S(1)} %constant_dynamic-slice_fusion.9, bf16[4,64,32,128]{3,2,1,0:T(8,128)(2,1)S(1)} %copy-done, s32[]{:T(128)S(6)} %copy.150), kind=kOutput, calls=%fused_computation.3.clone.1 | convolution fusion | flops 1086322688 | bytes 19408900 | tf_op jit(solution)/shard_map/while/body/eval_jaxpr/kqd,pkd->kqp/dot_general | solution.py:23
  54.7 8.1 %fusion.82 = f32[4,512]{1,0:T(4,128)S(1)} fusion(f32[4,512,2048]{2,1,0:T(8,128)} %get-tuple-element.325, f32[4,512]{1,0:T(4,128)S(1)} %get-tuple-element.324, pred[2048]{0:T(1024)(128)(4,1)S(1)} %add_compare_fusion.2), kind=kLoop, calls=%fused_computation.5.clone.1 | loop fusion | flops 20969472 | bytes 16795648 | tf_op jit(solution)/shard_map/while/body/eval_jaxpr/reduce_sum | solution.py:29
  63.1 0.9 constant_dynamic-slice_fusion.10
  63.9 0.7 fusion.83
  65.9 0.3 fusion.85
  66.2 0.9 constant_dynamic-slice_fusion.11
  67.1 0.4 convolution_bitcast_fusion.2
  67.5 2.0 constant_dynamic-slice_fusion.12
  69.5 7.7 %fusion.86 = f32[64,4,8,128]{3,2,0,1:T(8,128)S(1)} fusion(bf16[1,2048,4,128]{3,2,1,0:T(4,128)(2,1)S(1)} %constant_dynamic-slice_fusion.12, f32[4,512,2048]{2,1,0:T(8,128)} %get-tuple-element.325, f32[4,512]{1,0:T(4,128)S(1)} %get-tuple-element.324, pred[2048]{0:T(1024)(128)(4,1)S(1)} %add_compare_fusion.2), kind=kOutput, calls=%fused_computation.11.clone.1 | convolution fusion | flops 1094713344 | bytes 19933184 | tf_op jit(solution)/shard_map/while/body/eval_jaxpr/kqp,pkd->kqd/dot_general | solution.py:30
  77.1 1.6 bitcast_dynamic-update-slice_fusion.3
  79.5 1.5 dynamic_slice.82
  81.0 0.7 add_compare_fusion.2
  81.7 2.0 constant_dynamic-slice_fusion.9
  83.7 7.2 %fusion.81 = (f32[4,512]{1,0:T(4,128)S(1)}, f32[4,512,2048]{2,1,0:T(8,128)}) fusion(pred[2048]{0:T(1024)(128)(4,1)S(1)} %add_compare_fusion.2, bf16[1,2048,4,128]{3,2,1,0:T(4,128)(2,1)S(1)} %constant_dynamic-slice_fusion.9, bf16[4,64,32,128]{3,2,1,0:T(8,128)(2,1)S(1)} %copy-done, s32[]{:T(128)S(6)} %copy.150), kind=kOutput, calls=%fused_computation.3.clone.1 | convolution fusion | flops 1086322688 | bytes 19408900 | tf_op jit(solution)/shard_map/while/body/eval_jaxpr/kqd,pkd->kqp/dot_general | solution.py:23
  91.2 8.1 %fusion.82 = f32[4,512]{1,0:T(4,128)S(1)} fusion(f32[4,512,2048]{2,1,0:T(8,128)} %get-tuple-element.325, f32[4,512]{1,0:T(4,128)S(1)} %get-tuple-element.324, pred[2048]{0:T(1024)(128)(4,1)S(1)} %add_compare_fusion.2), kind=kLoop, calls=%fused_computation.5.clone.1 | loop fusion | flops 20969472 | bytes 16795648 | tf_op jit(solution)/shard_map/while/body/eval_jaxpr/reduce_sum | solution.py:29
  99.5 0.9 constant_dynamic-slice_fusion.10
  100.4 0.7 fusion.83
  102.4 0.3 fusion.85
  102.7 0.9 constant_dynamic-slice_fusion.11
  103.6 0.4 convolution_bitcast_fusion.2
  104.0 2.0 constant_dynamic-slice_fusion.12
  105.9 7.7 %fusion.86 = f32[64,4,8,128]{3,2,0,1:T(8,128)S(1)} fusion(bf16[1,2048,4,128]{3,2,1,0:T(4,128)(2,1)S(1)} %constant_dynamic-slice_fusion.12, f32[4,512,2048]{2,1,0:T(8,128)} %get-tuple-element.325, f32[4,512]{1,0:T(4,128)S(1)} %get-tuple-element.324, pred[2048]{0:T(1024)(128)(4,1)S(1)} %add_compare_fusion.2), kind=kOutput, calls=%fused_computation.11.clone.1 | convolution fusion | flops 1094713344 | bytes 19933184 | tf_op jit(solution)/shard_map/while/body/eval_jaxpr/kqp,pkd->kqd/dot_general | solution.py:30
  113.6 1.6 bitcast_dynamic-update-slice_fusion.3
  116.0 1.5 dynamic_slice.82
  117.4 0.7 add_compare_fusion.2
  118.1 2.0 constant_dynamic-slice_fusion.9
  120.1 7.2 %fusion.81 = (f32[4,512]{1,0:T(4,128)S(1)}, f32[4,512,2048]{2,1,0:T(8,128)}) fusion(pred[2048]{0:T(1024)(128)(4,1)S(1)} %add_compare_fusion.2, bf16[1,2048,4,128]{3,2,1,0:T(4,128)(2,1)S(1)} %constant_dynamic-slice_fusion.9, bf16[4,64,32,128]{3,2,1,0:T(8,128)(2,1)S(1)} %copy-done, s32[]{:T(128)S(6)} %copy.150), kind=kOutput, calls=%fused_computation.3.clone.1 | convolution fusion | flops 1086322688 | bytes 19408900 | tf_op jit(solution)/shard_map/while/body/eval_jaxpr/kqd,pkd->kqp/dot_general | solution.py:23
  127.6 8.1 %fusion.82 = f32[4,512]{1,0:T(4,128)S(1)} fusion(f32[4,512,2048]{2,1,0:T(8,128)} %get-tuple-element.325, f32[4,512]{1,0:T(4,128)S(1)} %get-tuple-element.324, pred[2048]{0:T(1024)(128)(4,1)S(1)} %add_compare_fusion.2), kind=kLoop, calls=%fused_computation.5.clone.1 | loop fusion | flops 20969472 | bytes 16795648 | tf_op jit(solution)/shard_map/while/body/eval_jaxpr/reduce_sum | solution.py:29
  136.0 0.9 constant_dynamic-slice_fusion.10
  136.9 0.7 fusion.83
  139.2 0.9 constant_dynamic-slice_fusion.11
  140.0 0.4 convolution_bitcast_fusion.2
  140.4 2.0 constant_dynamic-slice_fusion.12
  142.4 7.7 %fusion.86 = f32[64,4,8,128]{3,2,0,1:T(8,128)S(1)} fusion(bf16[1,2048,4,128]{3,2,1,0:T(4,128)(2,1)S(1)} %constant_dynamic-slice_fusion.12, f32[4,512,2048]{2,1,0:T(8,128)} %get-tuple-element.325, f32[4,512]{1,0:T(4,128)S(1)} %get-tuple-element.324, pred[2048]{0:T(1024)(128)(4,1)S(1)} %add_compare_fusion.2), kind=kOutput, calls=%fused_computation.11.clone.1 | convolution fusion | flops 1094713344 | bytes 19933184 | tf_op jit(solution)/shard_map/while/body/eval_jaxpr/kqp,pkd->kqd/dot_general | solution.py:30
  150.1 1.6 bitcast_dynamic-update-slice_fusion.3
  152.6 63.0 %pmax.7 = f32[256,32]{0,1:T(8,128)S(1)} all-reduce(f32[256,32]{0,1:T(8,128)S(1)} %reshape.69), channel_id=1, replica_groups=mesh['seq'=16,'head'=2] {'seq'}, use_global_device_ids=true, to_apply=%region_6.7 | all-reduce | flops 8192 | bytes 65536 | tf_op jit(solution)/shard_map/pmax | solution.py:86
  215.7 0.8 copy.68
  216.6 4.1 %bitcast_multiply_fusion = f32[256,32,128]{2,1,0:T(8,128)} fusion(f32[4,64,32,128]{3,2,1,0:T(8,128)} %get-tuple-element.87, f32[256,32]{1,0:T(8,128)S(1)} %copy.63), kind=kLoop, calls=%fused_computation.55 | loop fusion | flops 1048576 | bytes 8421376 | tf_op jit(solution)/shard_map/mul | solution.py:90
  221.0 48.6 %reduce-scatter.10.cloned.1.call-done = f32[16,32]{1,0:T(8,128)} async-done(((f32[256,32]{1,0:T(8,128)}), f32[16,32]{1,0:T(8,128)}) %reduce-scatter.10.cloned.1.call-update) | async-done | bytes 2064
  269.5 0.8 copy.69
  270.5 74.7 %reduce-scatter.6.cloned.1.call-done = f32[16,32,128]{2,1,0:T(8,128)} async-done(((f32[256,32,128]{2,1,0:T(8,128)}), f32[16,32,128]{2,1,0:T(8,128)}) %reduce-scatter.6.cloned.1.call-update) | async-done | bytes 262160 | tf_op jit(solution)/shard_map/reduce_scatter | solution.py:90
  345.2 1.2 divide_convert_fusion
  346.4 0.7 copy.112
  347.2 40.7 %all-gather.2.cloned.1.call-done = bf16[256,4096]{1,0:T(8,128)(2,1)} async-done(((bf16[16,4096]{1,0:T(8,128)(2,1)}), bf16[256,4096]{1,0:T(8,128)(2,1)}) %all-gather.2.cloned.1.call-update) | async-done | bytes 2097168 | tf_op jit(solution)/shard_map/all_gather | solution.py:105
  387.9 4.9 %fusion.35 = f32[256,512]{1,0:T(8,128)} fusion(bf16[256,4096]{1,0:T(8,128)(2,1)} %all-gather.2.cloned.1.call-done, bf16[4096,512]{1,0:T(8,128)(2,1)} %param.17), kind=kOutput, calls=%fused_computation.63 | convolution fusion | flops 1073741824 | bytes 6815744 | tf_op jit(solution)/shard_map/dot_general | solution.py:107
  392.8 13.5 %reduce-scatter.8.cloned.1.call-done = f32[128,512]{1,0:T(8,128)} async-done(((f32[256,512]{1,0:T(8,128)}), f32[128,512]{1,0:T(8,128)}) %reduce-scatter.8.cloned.1.call-update) | async-done | bytes 262160 | tf_op jit(solution)/shard_map/reduce_scatter | solution.py:106
  406.3 1.6 convert_element_type.19
  (116 shorter events, 11.1 us)
Async XLA Ops:
  6.5 263.0 %reduce-scatter.10.cloned.1.call-start = ((), (), s32[]{:S(2)}) async-start(), calls=%async_computation.6 | async-start | bytes 139264
  6.6 4.2 %copy-start = (bf16[4,64,32,128]{3,2,1,0:T(8,128)(2,1)S(1)}, bf16[4,64,32,128]{3,2,1,0:T(8,128)(2,1)}, u32[]{:S(2)}) copy-start(bf16[4,64,32,128]{3,2,1,0:T(8,128)(2,1)} %get-tuple-element.372) | copy-start | bytes 6291460 | tf_op jit(solution)/shard_map/while
  43.0 4.2 %copy-start = (bf16[4,64,32,128]{3,2,1,0:T(8,128)(2,1)S(1)}, bf16[4,64,32,128]{3,2,1,0:T(8,128)(2,1)}, u32[]{:S(2)}) copy-start(bf16[4,64,32,128]{3,2,1,0:T(8,128)(2,1)} %get-tuple-element.372) | copy-start | bytes 6291460 | tf_op jit(solution)/shard_map/while
  79.5 4.2 %copy-start = (bf16[4,64,32,128]{3,2,1,0:T(8,128)(2,1)S(1)}, bf16[4,64,32,128]{3,2,1,0:T(8,128)(2,1)}, u32[]{:S(2)}) copy-start(bf16[4,64,32,128]{3,2,1,0:T(8,128)(2,1)} %get-tuple-element.372) | copy-start | bytes 6291460 | tf_op jit(solution)/shard_map/while
  116.0 4.2 %copy-start = (bf16[4,64,32,128]{3,2,1,0:T(8,128)(2,1)S(1)}, bf16[4,64,32,128]{3,2,1,0:T(8,128)(2,1)}, u32[]{:S(2)}) copy-start(bf16[4,64,32,128]{3,2,1,0:T(8,128)(2,1)} %get-tuple-element.372) | copy-start | bytes 6291460 | tf_op jit(solution)/shard_map/while
  216.5 128.7 %reduce-scatter.6.cloned.1.call-start = ((), (), s32[]{:S(2)}) async-start(), calls=%async_computation.3 | async-start | bytes 4456448 | tf_op jit(solution)/shard_map/reduce_scatter | solution.py:90
  220.8 167.1 %all-gather.2.cloned.1.call-start = ((), (), s32[]{:S(2)}) async-start(), calls=%async_computation.4 | async-start | bytes 2228224 | tf_op jit(solution)/shard_map/all_gather | solution.py:105
  347.2 59.1 %reduce-scatter.8.cloned.1.call-start = ((), (), s32[]{:S(2)}) async-start(), calls=%async_computation.5 | async-start | bytes 786432 | tf_op jit(solution)/shard_map/reduce_scatter | solution.py:106
Sparse Core Ops, SparseCore 0:
  216.6 52.8 reduce-scatter.9
  273.4 71.7 reduce-scatter.5
  347.4 40.4 all-gather.1
  392.9 13.3 reduce-scatter.7
where the time goes:
time: 416 us; the launch traced here: 414 us
  waiting for transfers between devices  178 us (43%)
  matrix products  71.1 us (17%)
  blocking collectives  63 us (15%)
  local copies, waits for them, and re-layouts  46 us (11%)
  other arithmetic  42.7 us (10%)
  between operations  13.2 us (3%)
    reduce_scatter x1, waiting for transfers between devices, body(): lax.psum_scatter(cache_acc * factor[..., None], 'seq', scatter_dimension=...  74.7 us
    pmax x1, blocking collectives, body(): overall = lax.pmax(cache_max, 'seq')  63 us
    unnamed x5, waiting for transfers between devices  48.6 us
    all_gather x1, waiting for transfers between devices, body(): attended = lax.all_gather(share, 'seq', axis=0, tiled=True)  40.7 us
    reduce_sum x8, other arithmetic, partial_scores(): totals = jnp.sum(weights, axis=-1)  32.9 us
    dot_general x8, matrix products, partial_scores(): jnp.einsum('kqp,pkd->kqd', weights.astype(jnp.bfloat16), values, preferre...  32.1 us
    dot_general x8, matrix products, partial_scores(): jnp.einsum('kqd,pkd->kqp', query_rows, keys, preferred_element_type=jnp.f...  30 us
    dynamic_slice x20, local copies, waits for them, and re-layouts, body(): lax.map(one_request, (queries, new_keys, new_values, cache_keys, cache_va...  28.8 us
  transfers between devices with their start and end apart: 4, of which 4 were waited for; matrix products, arithmetic and copies ran while one was open for 1% of the time, Pallas kernels for 0%

commit v1 on v0

--- a/solution.py
+++ b/solution.py
@@ -102,7 +102,12 @@
     share = (
         (weighted / totals[..., None]).astype(jnp.bfloat16).reshape(row_count, heads * head_size)
     )
-    attended = lax.all_gather(share, "seq", axis=0, tiled=True)
+    ring = [share]
+    for hop in range(15):
+        ring.append(lax.ppermute(ring[-1], "seq", [(dev, (dev + 1) % 16) for dev in range(16)]))
+    attended = jnp.roll(
+        jnp.concatenate(ring[::-1], axis=0), (lax.axis_index("seq") + 1) * ring[0].shape[0], axis=0
+    )
     mixed = lax.psum_scatter(
         jnp.dot(attended, out_weight, preferred_element_type=jnp.float32),
         "head",

time: 416 us -> 477 us (1.15)
  waiting for transfers between devices: 178 us -> 242 us
    ppermute x0 -> x15, waiting for transfers between devices: none -> 106 us  [body(): lax.ppermute(ring[-1], 'seq', [(dev, (dev + 1) % 16) for dev in range(16)])]
    all_gather x1 -> x0, waiting for transfers between devices: 40.7 us -> none  [body(): attended = lax.all_gather(share, 'seq', axis=0, tiled=True)]
    unnamed x5 -> x4, waiting for transfers between devices: 48.6 us -> 48.6 us
  transfers between devices with their start and end apart: 4 -> 18, of which waited for: 4 -> 18; matrix products, arithmetic and copies ran while one was open for 1% -> 1% of each run, Pallas kernels for 0% -> 0%
where the time goes in v1:
time: 477 us; the launch traced here: 476 us
  waiting for transfers between devices  242 us (51%)
  matrix products  68.4 us (14%)
  blocking collectives  63 us (13%)
  local copies, waits for them, and re-layouts  45.7 us (10%)
  other arithmetic  42.7 us (9%)
  between operations  13.4 us (3%)
    ppermute x15, waiting for transfers between devices, body(): lax.ppermute(ring[-1], 'seq', [(dev, (dev + 1) % 16) for dev in range(16)])  106 us
    reduce_scatter x1, waiting for transfers between devices, body(): lax.psum_scatter(cache_acc * factor[..., None], 'seq', scatter_dimension=...  74.8 us
    pmax x1, blocking collectives, body(): overall = lax.pmax(cache_max, 'seq')  63 us
    unnamed x4, waiting for transfers between devices  48.6 us
    reduce_sum x8, other arithmetic, partial_scores(): totals = jnp.sum(weights, axis=-1)  32.9 us
    dot_general x8, matrix products, partial_scores(): jnp.einsum('kqp,pkd->kqd', weights.astype(jnp.bfloat16), values, preferre...  32.1 us
    dot_general x8, matrix products, partial_scores(): jnp.einsum('kqd,pkd->kqp', query_rows, keys, preferred_element_type=jnp.f...  30.1 us
    dynamic_slice x20, local copies, waits for them, and re-layouts, body(): lax.map(one_request, (queries, new_keys, new_values, cache_keys, cache_va...  28.7 us
  transfers between devices with their start and end apart: 18, of which 18 were waited for; matrix products, arithmetic and copies ran while one was open for 1% of the time, Pallas kernels for 0%

profile of v1, /device:TPU:0, one launch (start us, length us, event | category | flops | bytes accessed | tf_op | source)
XLA Modules:
  0.0 475.9 jit_solution(11823134101304719582)
XLA Ops:
  6.5 145.9 %while.21 = (s32[]{:T(128)}, f32[4,64,32]{1,0,2:T(4,128)S(1)}, f32[4,64,32]{1,0,2:T(4,128)S(1)}, f32[4,64,32,128]{3,2,1,0:T(8,128)}, f32[4,64,32]{1,0,2:T(4,128)...) while((s32[]{:T(128)}, f32[4,64,32]{1,0,2:T(4,128)S(1)}, ...), condition=%wide.region_5.6_spmd.clone, body=%wide.region_0.5_spmd.clone.sunk | while | flops 2289217536 | bytes 81249280 | solution.py:77
  6.6 1.5 dynamic_slice.89
  8.7 2.0 constant_dynamic-slice_fusion.9
  10.7 7.2 %fusion.82 = (f32[4,512]{1,0:T(4,128)S(1)}, f32[4,512,2048]{2,1,0:T(8,128)}) fusion(pred[2048]{0:T(1024)(128)(4,1)S(1)} %add_compare_fusion.2, bf16[1,2048,4,128]{3,2,1,0:T(4,128)(2,1)S(1)} %constant_dynamic-slice_fusion.9, bf16[4,64,32,128]{3,2,1,0:T(8,128)(2,1)S(1)} %copy-done, s32[]{:T(128)S(6)} %copy.154), kind=kOutput, calls=%fused_computation.3.clone.1 | convolution fusion | flops 1086322688 | bytes 19408900 | tf_op jit(solution)/shard_map/while/body/eval_jaxpr/kqd,pkd->kqp/dot_general | solution.py:23
  18.2 8.1 %fusion.83 = f32[4,512]{1,0:T(4,128)S(1)} fusion(f32[4,512,2048]{2,1,0:T(8,128)} %get-tuple-element.325, f32[4,512]{1,0:T(4,128)S(1)} %get-tuple-element.324, pred[2048]{0:T(1024)(128)(4,1)S(1)} %add_compare_fusion.2), kind=kLoop, calls=%fused_computation.5.clone.1 | loop fusion | flops 20969472 | bytes 16795648 | tf_op jit(solution)/shard_map/while/body/eval_jaxpr/reduce_sum | solution.py:29
  26.6 0.9 constant_dynamic-slice_fusion.10
  27.5 0.7 fusion.84
  29.8 0.9 constant_dynamic-slice_fusion.11
  31.0 2.0 constant_dynamic-slice_fusion.12
  33.0 7.7 %fusion.87 = f32[64,4,8,128]{3,2,0,1:T(8,128)S(1)} fusion(bf16[1,2048,4,128]{3,2,1,0:T(4,128)(2,1)S(1)} %constant_dynamic-slice_fusion.12, f32[4,512,2048]{2,1,0:T(8,128)} %get-tuple-element.325, f32[4,512]{1,0:T(4,128)S(1)} %get-tuple-element.324, pred[2048]{0:T(1024)(128)(4,1)S(1)} %add_compare_fusion.2), kind=kOutput, calls=%fused_computation.11.clone.1 | convolution fusion | flops 1094713344 | bytes 19933184 | tf_op jit(solution)/shard_map/while/body/eval_jaxpr/kqp,pkd->kqd/dot_general | solution.py:30
  40.7 1.6 bitcast_dynamic-update-slice_fusion.3
  43.0 1.5 dynamic_slice.89
  45.2 2.0 constant_dynamic-slice_fusion.9
  47.2 7.2 %fusion.82 = (f32[4,512]{1,0:T(4,128)S(1)}, f32[4,512,2048]{2,1,0:T(8,128)}) fusion(pred[2048]{0:T(1024)(128)(4,1)S(1)} %add_compare_fusion.2, bf16[1,2048,4,128]{3,2,1,0:T(4,128)(2,1)S(1)} %constant_dynamic-slice_fusion.9, bf16[4,64,32,128]{3,2,1,0:T(8,128)(2,1)S(1)} %copy-done, s32[]{:T(128)S(6)} %copy.154), kind=kOutput, calls=%fused_computation.3.clone.1 | convolution fusion | flops 1086322688 | bytes 19408900 | tf_op jit(solution)/shard_map/while/body/eval_jaxpr/kqd,pkd->kqp/dot_general | solution.py:23
  54.7 8.1 %fusion.83 = f32[4,512]{1,0:T(4,128)S(1)} fusion(f32[4,512,2048]{2,1,0:T(8,128)} %get-tuple-element.325, f32[4,512]{1,0:T(4,128)S(1)} %get-tuple-element.324, pred[2048]{0:T(1024)(128)(4,1)S(1)} %add_compare_fusion.2), kind=kLoop, calls=%fused_computation.5.clone.1 | loop fusion | flops 20969472 | bytes 16795648 | tf_op jit(solution)/shard_map/while/body/eval_jaxpr/reduce_sum | solution.py:29
  63.1 0.9 constant_dynamic-slice_fusion.10
  66.2 0.9 constant_dynamic-slice_fusion.11
  67.5 2.0 constant_dynamic-slice_fusion.12
  69.5 7.7 %fusion.87 = f32[64,4,8,128]{3,2,0,1:T(8,128)S(1)} fusion(bf16[1,2048,4,128]{3,2,1,0:T(4,128)(2,1)S(1)} %constant_dynamic-slice_fusion.12, f32[4,512,2048]{2,1,0:T(8,128)} %get-tuple-element.325, f32[4,512]{1,0:T(4,128)S(1)} %get-tuple-element.324, pred[2048]{0:T(1024)(128)(4,1)S(1)} %add_compare_fusion.2), kind=kOutput, calls=%fused_computation.11.clone.1 | convolution fusion | flops 1094713344 | bytes 19933184 | tf_op jit(solution)/shard_map/while/body/eval_jaxpr/kqp,pkd->kqd/dot_general | solution.py:30
  77.1 1.6 bitcast_dynamic-update-slice_fusion.3
  79.5 1.5 dynamic_slice.89
  81.6 2.0 constant_dynamic-slice_fusion.9
  83.7 7.2 %fusion.82 = (f32[4,512]{1,0:T(4,128)S(1)}, f32[4,512,2048]{2,1,0:T(8,128)}) fusion(pred[2048]{0:T(1024)(128)(4,1)S(1)} %add_compare_fusion.2, bf16[1,2048,4,128]{3,2,1,0:T(4,128)(2,1)S(1)} %constant_dynamic-slice_fusion.9, bf16[4,64,32,128]{3,2,1,0:T(8,128)(2,1)S(1)} %copy-done, s32[]{:T(128)S(6)} %copy.154), kind=kOutput, calls=%fused_computation.3.clone.1 | convolution fusion | flops 1086322688 | bytes 19408900 | tf_op jit(solution)/shard_map/while/body/eval_jaxpr/kqd,pkd->kqp/dot_general | solution.py:23
  91.2 8.1 %fusion.83 = f32[4,512]{1,0:T(4,128)S(1)} fusion(f32[4,512,2048]{2,1,0:T(8,128)} %get-tuple-element.325, f32[4,512]{1,0:T(4,128)S(1)} %get-tuple-element.324, pred[2048]{0:T(1024)(128)(4,1)S(1)} %add_compare_fusion.2), kind=kLoop, calls=%fused_computation.5.clone.1 | loop fusion | flops 20969472 | bytes 16795648 | tf_op jit(solution)/shard_map/while/body/eval_jaxpr/reduce_sum | solution.py:29
  99.5 0.9 constant_dynamic-slice_fusion.10
  102.7 0.9 constant_dynamic-slice_fusion.11
  104.0 2.0 constant_dynamic-slice_fusion.12
  105.9 7.7 %fusion.87 = f32[64,4,8,128]{3,2,0,1:T(8,128)S(1)} fusion(bf16[1,2048,4,128]{3,2,1,0:T(4,128)(2,1)S(1)} %constant_dynamic-slice_fusion.12, f32[4,512,2048]{2,1,0:T(8,128)} %get-tuple-element.325, f32[4,512]{1,0:T(4,128)S(1)} %get-tuple-element.324, pred[2048]{0:T(1024)(128)(4,1)S(1)} %add_compare_fusion.2), kind=kOutput, calls=%fused_computation.11.clone.1 | convolution fusion | flops 1094713344 | bytes 19933184 | tf_op jit(solution)/shard_map/while/body/eval_jaxpr/kqp,pkd->kqd/dot_general | solution.py:30
  113.6 1.6 bitcast_dynamic-update-slice_fusion.3
  116.0 1.5 dynamic_slice.89
  118.1 2.0 constant_dynamic-slice_fusion.9
  120.1 7.2 %fusion.82 = (f32[4,512]{1,0:T(4,128)S(1)}, f32[4,512,2048]{2,1,0:T(8,128)}) fusion(pred[2048]{0:T(1024)(128)(4,1)S(1)} %add_compare_fusion.2, bf16[1,2048,4,128]{3,2,1,0:T(4,128)(2,1)S(1)} %constant_dynamic-slice_fusion.9, bf16[4,64,32,128]{3,2,1,0:T(8,128)(2,1)S(1)} %copy-done, s32[]{:T(128)S(6)} %copy.154), kind=kOutput, calls=%fused_computation.3.clone.1 | convolution fusion | flops 1086322688 | bytes 19408900 | tf_op jit(solution)/shard_map/while/body/eval_jaxpr/kqd,pkd->kqp/dot_general | solution.py:23
  127.6 8.1 %fusion.83 = f32[4,512]{1,0:T(4,128)S(1)} fusion(f32[4,512,2048]{2,1,0:T(8,128)} %get-tuple-element.325, f32[4,512]{1,0:T(4,128)S(1)} %get-tuple-element.324, pred[2048]{0:T(1024)(128)(4,1)S(1)} %add_compare_fusion.2), kind=kLoop, calls=%fused_computation.5.clone.1 | loop fusion | flops 20969472 | bytes 16795648 | tf_op jit(solution)/shard_map/while/body/eval_jaxpr/reduce_sum | solution.py:29
  136.0 0.9 constant_dynamic-slice_fusion.10
  136.9 0.7 fusion.84
  139.2 0.9 constant_dynamic-slice_fusion.11
  140.4 2.0 constant_dynamic-slice_fusion.12
  142.4 7.7 %fusion.87 = f32[64,4,8,128]{3,2,0,1:T(8,128)S(1)} fusion(bf16[1,2048,4,128]{3,2,1,0:T(4,128)(2,1)S(1)} %constant_dynamic-slice_fusion.12, f32[4,512,2048]{2,1,0:T(8,128)} %get-tuple-element.325, f32[4,512]{1,0:T(4,128)S(1)} %get-tuple-element.324, pred[2048]{0:T(1024)(128)(4,1)S(1)} %add_compare_fusion.2), kind=kOutput, calls=%fused_computation.11.clone.1 | convolution fusion | flops 1094713344 | bytes 19933184 | tf_op jit(solution)/shard_map/while/body/eval_jaxpr/kqp,pkd->kqd/dot_general | solution.py:30
  150.1 1.6 bitcast_dynamic-update-slice_fusion.3
  152.6 63.0 %pmax.7 = f32[256,32]{0,1:T(8,128)S(1)} all-reduce(f32[256,32]{0,1:T(8,128)S(1)} %reshape.69), channel_id=1, replica_groups=mesh['seq'=16,'head'=2] {'seq'}, use_global_device_ids=true, to_apply=%region_6.7 | all-reduce | flops 8192 | bytes 65536 | tf_op jit(solution)/shard_map/pmax | solution.py:86
  215.7 0.8 copy.68
  216.6 4.2 bitcast_multiply_fusion
  221.0 48.5 %reduce-scatter.10.cloned.1.call-done = f32[16,32]{1,0:T(8,128)} async-done(((f32[256,32]{1,0:T(8,128)}), f32[16,32]{1,0:T(8,128)}) %reduce-scatter.10.cloned.1.call-update) | async-done | bytes 2064
  269.5 0.8 copy.69
  270.5 74.8 %reduce-scatter.6.cloned.1.call-done = f32[16,32,128]{2,1,0:T(8,128)} async-done(((f32[256,32,128]{2,1,0:T(8,128)}), f32[16,32,128]{2,1,0:T(8,128)}) %reduce-scatter.6.cloned.1.call-update) | async-done | bytes 262160 | tf_op jit(solution)/shard_map/reduce_scatter | solution.py:90
  345.3 1.2 divide_convert_fusion
  346.6 7.1 %collective-permute-done = bf16[16,4096]{1,0:T(8,128)(2,1)S(1)} collective-permute-done((bf16[16,4096]{1,0:T(8,128)(2,1)S(1)}, bf16[16,4096]{1,0:T(8,128)(2,1)S(1)}, u32[]{:S(2)}, u32[]{:S(2)}) %collective-permute-start) | collective-permute-done | bytes 131104 | tf_op jit(solution)/shard_map/ppermute | solution.py:107
  353.7 7.1 %collective-permute-done.1 = bf16[16,4096]{1,0:T(8,128)(2,1)S(1)} collective-permute-done((bf16[16,4096]{1,0:T(8,128)(2,1)S(1)}, bf16[16,4096]{1,0:T(8,128)(2,1)S(1)}, u32[]{:S(2)}, u32[]{:S(2)}) %collective-permute-start.1) | collective-permute-done | bytes 131104 | tf_op jit(solution)/shard_map/ppermute | solution.py:107
  360.8 7.1 %collective-permute-done.2 = bf16[16,4096]{1,0:T(8,128)(2,1)S(1)} collective-permute-done((bf16[16,4096]{1,0:T(8,128)(2,1)S(1)}, bf16[16,4096]{1,0:T(8,128)(2,1)S(1)}, u32[]{:S(2)}, u32[]{:S(2)}) %collective-permute-start.2) | collective-permute-done | bytes 131104 | tf_op jit(solution)/shard_map/ppermute | solution.py:107
  367.9 7.1 %collective-permute-done.3 = bf16[16,4096]{1,0:T(8,128)(2,1)S(1)} collective-permute-done((bf16[16,4096]{1,0:T(8,128)(2,1)S(1)}, bf16[16,4096]{1,0:T(8,128)(2,1)S(1)}, u32[]{:S(2)}, u32[]{:S(2)}) %collective-permute-start.3) | collective-permute-done | bytes 131104 | tf_op jit(solution)/shard_map/ppermute | solution.py:107
  375.0 7.1 %collective-permute-done.4 = bf16[16,4096]{1,0:T(8,128)(2,1)S(1)} collective-permute-done((bf16[16,4096]{1,0:T(8,128)(2,1)S(1)}, bf16[16,4096]{1,0:T(8,128)(2,1)S(1)}, u32[]{:S(2)}, u32[]{:S(2)}) %collective-permute-start.4) | collective-permute-done | bytes 131104 | tf_op jit(solution)/shard_map/ppermute | solution.py:107
  382.1 7.1 %collective-permute-done.5 = bf16[16,4096]{1,0:T(8,128)(2,1)S(1)} collective-permute-done((bf16[16,4096]{1,0:T(8,128)(2,1)S(1)}, bf16[16,4096]{1,0:T(8,128)(2,1)S(1)}, u32[]{:S(2)}, u32[]{:S(2)}) %collective-permute-start.5) | collective-permute-done | bytes 131104 | tf_op jit(solution)/shard_map/ppermute | solution.py:107
  389.2 7.1 %collective-permute-done.6 = bf16[16,4096]{1,0:T(8,128)(2,1)S(1)} collective-permute-done((bf16[16,4096]{1,0:T(8,128)(2,1)S(1)}, bf16[16,4096]{1,0:T(8,128)(2,1)S(1)}, u32[]{:S(2)}, u32[]{:S(2)}) %collective-permute-start.6) | collective-permute-done | bytes 131104 | tf_op jit(solution)/shard_map/ppermute | solution.py:107
  396.2 7.1 %collective-permute-done.7 = bf16[16,4096]{1,0:T(8,128)(2,1)S(1)} collective-permute-done((bf16[16,4096]{1,0:T(8,128)(2,1)S(1)}, bf16[16,4096]{1,0:T(8,128)(2,1)S(1)}, u32[]{:S(2)}, u32[]{:S(2)}) %collective-permute-start.7) | collective-permute-done | bytes 131104 | tf_op jit(solution)/shard_map/ppermute | solution.py:107
  403.3 7.1 %collective-permute-done.8 = bf16[16,4096]{1,0:T(8,128)(2,1)S(1)} collective-permute-done((bf16[16,4096]{1,0:T(8,128)(2,1)S(1)}, bf16[16,4096]{1,0:T(8,128)(2,1)S(1)}, u32[]{:S(2)}, u32[]{:S(2)}) %collective-permute-start.8) | collective-permute-done | bytes 131104 | tf_op jit(solution)/shard_map/ppermute | solution.py:107
  410.4 7.1 %collective-permute-done.9 = bf16[16,4096]{1,0:T(8,128)(2,1)S(1)} collective-permute-done((bf16[16,4096]{1,0:T(8,128)(2,1)S(1)}, bf16[16,4096]{1,0:T(8,128)(2,1)S(1)}, u32[]{:S(2)}, u32[]{:S(2)}) %collective-permute-start.9) | collective-permute-done | bytes 131104 | tf_op jit(solution)/shard_map/ppermute | solution.py:107
  417.5 7.1 %collective-permute-done.10 = bf16[16,4096]{1,0:T(8,128)(2,1)S(1)} collective-permute-done((bf16[16,4096]{1,0:T(8,128)(2,1)S(1)}, bf16[16,4096]{1,0:T(8,128)(2,1)S(1)}, u32[]{:S(2)}, u32[]{:S(2)}) %collective-permute-start.10) | collective-permute-done | bytes 131104 | tf_op jit(solution)/shard_map/ppermute | solution.py:107
  424.6 7.1 %collective-permute-done.11 = bf16[16,4096]{1,0:T(8,128)(2,1)S(1)} collective-permute-done((bf16[16,4096]{1,0:T(8,128)(2,1)S(1)}, bf16[16,4096]{1,0:T(8,128)(2,1)S(1)}, u32[]{:S(2)}, u32[]{:S(2)}) %collective-permute-start.11) | collective-permute-done | bytes 131104 | tf_op jit(solution)/shard_map/ppermute | solution.py:107
  431.7 7.1 %collective-permute-done.12 = bf16[16,4096]{1,0:T(8,128)(2,1)S(1)} collective-permute-done((bf16[16,4096]{1,0:T(8,128)(2,1)S(1)}, bf16[16,4096]{1,0:T(8,128)(2,1)S(1)}, u32[]{:S(2)}, u32[]{:S(2)}) %collective-permute-start.12) | collective-permute-done | bytes 131104 | tf_op jit(solution)/shard_map/ppermute | solution.py:107
  438.8 7.1 %collective-permute-done.13 = bf16[16,4096]{1,0:T(8,128)(2,1)S(1)} collective-permute-done((bf16[16,4096]{1,0:T(8,128)(2,1)S(1)}, bf16[16,4096]{1,0:T(8,128)(2,1)S(1)}, u32[]{:S(2)}, u32[]{:S(2)}) %collective-permute-start.13) | collective-permute-done | bytes 131104 | tf_op jit(solution)/shard_map/ppermute | solution.py:107
  445.9 7.1 %collective-permute-done.14 = bf16[16,4096]{1,0:T(8,128)(2,1)S(1)} collective-permute-done((bf16[16,4096]{1,0:T(8,128)(2,1)S(1)}, bf16[16,4096]{1,0:T(8,128)(2,1)S(1)}, u32[]{:S(2)}, u32[]{:S(2)}) %collective-permute-start.14) | collective-permute-done | bytes 131104 | tf_op jit(solution)/shard_map/ppermute | solution.py:107
  453.6 2.1 fusion.33
  455.7 12.0 %reduce-scatter.8.cloned.1.call-done = f32[128,512]{1,0:T(8,128)} async-done(((f32[256,512]{1,0:T(8,128)}), f32[128,512]{1,0:T(8,128)}) %reduce-scatter.8.cloned.1.call-update) | async-done | bytes 262160 | tf_op jit(solution)/shard_map/reduce_scatter | solution.py:111
  467.7 1.6 convert_element_type.19
  (177 shorter events, 18.1 us)
Async XLA Ops:
  6.5 263.0 %reduce-scatter.10.cloned.1.call-start = ((), (), s32[]{:S(2)}) async-start(), calls=%async_computation.5 | async-start | bytes 139264
  6.6 4.2 copy-start
  43.0 4.2 copy-start
  79.5 4.2 copy-start
  115.9 4.2 copy-start
  216.5 128.8 %reduce-scatter.6.cloned.1.call-start = ((), (), s32[]{:S(2)}) async-start(), calls=%async_computation.3 | async-start | bytes 4456448 | tf_op jit(solution)/shard_map/reduce_scatter | solution.py:90
  220.8 246.9 %reduce-scatter.8.cloned.1.call-start = ((), (), s32[]{:S(2)}) async-start(), calls=%async_computation.4 | async-start | bytes 786432 | tf_op jit(solution)/shard_map/reduce_scatter | solution.py:111
  346.6 7.1 %collective-permute-start = (bf16[16,4096]{1,0:T(8,128)(2,1)S(1)}, bf16[16,4096]{1,0:T(8,128)(2,1)S(1)}, u32[]{:S(2)}, u32[]{:S(2)}) collective-permute-start(bf16[16,4096]{1,0:T(8,128)(2,1)S(1)} %bitcast.174), channel_id=1, source_target_pairs={{0,2},{2,4},{4,6},{6,8},{8,10},{10,12},{12,14},{14,16},{16,18},{18... | collective-permute-start | bytes 393224 | tf_op jit(solution)/shard_map/ppermute | solution.py:107
  353.7 7.1 %collective-permute-start.1 = (bf16[16,4096]{1,0:T(8,128)(2,1)S(1)}, bf16[16,4096]{1,0:T(8,128)(2,1)S(1)}, u32[]{:S(2)}, u32[]{:S(2)}) collective-permute-start(bf16[16,4096]{1,0:T(8,128)(2,1)S(1)} %collective-permute-done), channel_id=1, source_target_pairs={{0,2},{2,4},{4,6},{6,8},{8,10},{10,12},{12,14},{14,16},{16,18},{18... | collective-permute-start | bytes 393224 | tf_op jit(solution)/shard_map/ppermute | solution.py:107
  360.8 7.1 %collective-permute-start.2 = (bf16[16,4096]{1,0:T(8,128)(2,1)S(1)}, bf16[16,4096]{1,0:T(8,128)(2,1)S(1)}, u32[]{:S(2)}, u32[]{:S(2)}) collective-permute-start(bf16[16,4096]{1,0:T(8,128)(2,1)S(1)} %collective-permute-done.1), channel_id=1, source_target_pairs={{0,2},{2,4},{4,6},{6,8},{8,10},{10,12},{12,14},{14,16},{16,18},{18... | collective-permute-start | bytes 393224 | tf_op jit(solution)/shard_map/ppermute | solution.py:107
  367.9 7.1 %collective-permute-start.3 = (bf16[16,4096]{1,0:T(8,128)(2,1)S(1)}, bf16[16,4096]{1,0:T(8,128)(2,1)S(1)}, u32[]{:S(2)}, u32[]{:S(2)}) collective-permute-start(bf16[16,4096]{1,0:T(8,128)(2,1)S(1)} %collective-permute-done.2), channel_id=1, source_target_pairs={{0,2},{2,4},{4,6},{6,8},{8,10},{10,12},{12,14},{14,16},{16,18},{18... | collective-permute-start | bytes 393224 | tf_op jit(solution)/shard_map/ppermute | solution.py:107
  375.0 7.1 %collective-permute-start.4 = (bf16[16,4096]{1,0:T(8,128)(2,1)S(1)}, bf16[16,4096]{1,0:T(8,128)(2,1)S(1)}, u32[]{:S(2)}, u32[]{:S(2)}) collective-permute-start(bf16[16,4096]{1,0:T(8,128)(2,1)S(1)} %collective-permute-done.3), channel_id=1, source_target_pairs={{0,2},{2,4},{4,6},{6,8},{8,10},{10,12},{12,14},{14,16},{16,18},{18... | collective-permute-start | bytes 393224 | tf_op jit(solution)/shard_map/ppermute | solution.py:107
  382.1 7.1 %collective-permute-start.5 = (bf16[16,4096]{1,0:T(8,128)(2,1)S(1)}, bf16[16,4096]{1,0:T(8,128)(2,1)S(1)}, u32[]{:S(2)}, u32[]{:S(2)}) collective-permute-start(bf16[16,4096]{1,0:T(8,128)(2,1)S(1)} %collective-permute-done.4), channel_id=1, source_target_pairs={{0,2},{2,4},{4,6},{6,8},{8,10},{10,12},{12,14},{14,16},{16,18},{18... | collective-permute-start | bytes 393224 | tf_op jit(solution)/shard_map/ppermute | solution.py:107
  389.2 7.1 %collective-permute-start.6 = (bf16[16,4096]{1,0:T(8,128)(2,1)S(1)}, bf16[16,4096]{1,0:T(8,128)(2,1)S(1)}, u32[]{:S(2)}, u32[]{:S(2)}) collective-permute-start(bf16[16,4096]{1,0:T(8,128)(2,1)S(1)} %collective-permute-done.5), channel_id=1, source_target_pairs={{0,2},{2,4},{4,6},{6,8},{8,10},{10,12},{12,14},{14,16},{16,18},{18... | collective-permute-start | bytes 393224 | tf_op jit(solution)/shard_map/ppermute | solution.py:107
  396.2 7.1 %collective-permute-start.7 = (bf16[16,4096]{1,0:T(8,128)(2,1)S(1)}, bf16[16,4096]{1,0:T(8,128)(2,1)S(1)}, u32[]{:S(2)}, u32[]{:S(2)}) collective-permute-start(bf16[16,4096]{1,0:T(8,128)(2,1)S(1)} %collective-permute-done.6), channel_id=1, source_target_pairs={{0,2},{2,4},{4,6},{6,8},{8,10},{10,12},{12,14},{14,16},{16,18},{18... | collective-permute-start | bytes 393224 | tf_op jit(solution)/shard_map/ppermute | solution.py:107
  403.3 7.1 %collective-permute-start.8 = (bf16[16,4096]{1,0:T(8,128)(2,1)S(1)}, bf16[16,4096]{1,0:T(8,128)(2,1)S(1)}, u32[]{:S(2)}, u32[]{:S(2)}) collective-permute-start(bf16[16,4096]{1,0:T(8,128)(2,1)S(1)} %collective-permute-done.7), channel_id=1, source_target_pairs={{0,2},{2,4},{4,6},{6,8},{8,10},{10,12},{12,14},{14,16},{16,18},{18... | collective-permute-start | bytes 393224 | tf_op jit(solution)/shard_map/ppermute | solution.py:107
  410.4 7.1 %collective-permute-start.9 = (bf16[16,4096]{1,0:T(8,128)(2,1)S(1)}, bf16[16,4096]{1,0:T(8,128)(2,1)S(1)}, u32[]{:S(2)}, u32[]{:S(2)}) collective-permute-start(bf16[16,4096]{1,0:T(8,128)(2,1)S(1)} %collective-permute-done.8), channel_id=1, source_target_pairs={{0,2},{2,4},{4,6},{6,8},{8,10},{10,12},{12,14},{14,16},{16,18},{18... | collective-permute-start | bytes 393224 | tf_op jit(solution)/shard_map/ppermute | solution.py:107
  417.5 7.1 %collective-permute-start.10 = (bf16[16,4096]{1,0:T(8,128)(2,1)S(1)}, bf16[16,4096]{1,0:T(8,128)(2,1)S(1)}, u32[]{:S(2)}, u32[]{:S(2)}) collective-permute-start(bf16[16,4096]{1,0:T(8,128)(2,1)S(1)} %collective-permute-done.9), channel_id=1, source_target_pairs={{0,2},{2,4},{4,6},{6,8},{8,10},{10,12},{12,14},{14,16},{16,18},{18... | collective-permute-start | bytes 393224 | tf_op jit(solution)/shard_map/ppermute | solution.py:107
  424.6 7.1 %collective-permute-start.11 = (bf16[16,4096]{1,0:T(8,128)(2,1)S(1)}, bf16[16,4096]{1,0:T(8,128)(2,1)S(1)}, u32[]{:S(2)}, u32[]{:S(2)}) collective-permute-start(bf16[16,4096]{1,0:T(8,128)(2,1)S(1)} %collective-permute-done.10), channel_id=1, source_target_pairs={{0,2},{2,4},{4,6},{6,8},{8,10},{10,12},{12,14},{14,16},{16,18},{18... | collective-permute-start | bytes 393224 | tf_op jit(solution)/shard_map/ppermute | solution.py:107
  431.7 7.1 %collective-permute-start.12 = (bf16[16,4096]{1,0:T(8,128)(2,1)S(1)}, bf16[16,4096]{1,0:T(8,128)(2,1)S(1)}, u32[]{:S(2)}, u32[]{:S(2)}) collective-permute-start(bf16[16,4096]{1,0:T(8,128)(2,1)S(1)} %collective-permute-done.11), channel_id=1, source_target_pairs={{0,2},{2,4},{4,6},{6,8},{8,10},{10,12},{12,14},{14,16},{16,18},{18... | collective-permute-start | bytes 393224 | tf_op jit(solution)/shard_map/ppermute | solution.py:107
  438.8 7.1 %collective-permute-start.13 = (bf16[16,4096]{1,0:T(8,128)(2,1)S(1)}, bf16[16,4096]{1,0:T(8,128)(2,1)S(1)}, u32[]{:S(2)}, u32[]{:S(2)}) collective-permute-start(bf16[16,4096]{1,0:T(8,128)(2,1)S(1)} %collective-permute-done.12), channel_id=1, source_target_pairs={{0,2},{2,4},{4,6},{6,8},{8,10},{10,12},{12,14},{14,16},{16,18},{18... | collective-permute-start | bytes 393224 | tf_op jit(solution)/shard_map/ppermute | solution.py:107
  445.9 7.1 %collective-permute-start.14 = (bf16[16,4096]{1,0:T(8,128)(2,1)S(1)}, bf16[16,4096]{1,0:T(8,128)(2,1)S(1)}, u32[]{:S(2)}, u32[]{:S(2)}) collective-permute-start(bf16[16,4096]{1,0:T(8,128)(2,1)S(1)} %collective-permute-done.13), channel_id=1, source_target_pairs={{0,2},{2,4},{4,6},{6,8},{8,10},{10,12},{12,14},{14,16},{16,18},{18... | collective-permute-start | bytes 393224 | tf_op jit(solution)/shard_map/ppermute | solution.py:107
  445.9 7.8 %copy-start.1 = (bf16[4096,512]{1,0:T(8,128)(2,1)S(1)}, bf16[4096,512]{1,0:T(8,128)(2,1)}, u32[]{:S(2)}) copy-start(bf16[4096,512]{1,0:T(8,128)(2,1)} %param.17) | copy-start | bytes 12582916
Sparse Core Ops, SparseCore 0:
  216.6 52.8 reduce-scatter.9
  273.4 71.8 reduce-scatter.5
  455.8 11.8 reduce-scatter.7
